TPU v7x, 32 devices: a whole 2x2x4 slice. The times are simulated.
32 devices in a mesh: space: 8 (over z, y), fsdp: 4 (over x, core).
Axes of the slice: x: 2, y: 2, z: 4, core: 2. Of those that a mesh axis runs over, the one named last changes fastest.
Arguments:
- features: bfloat16 [8, 4, 384, 384], P('space', 'fsdp'), may hold values from -60 to 60
- channel_gain: float32 [384], replicated, may hold values from 0.5 to 2
- conv_weight: bfloat16 [27, 384, 384], P(None, 'space', 'fsdp'), may hold values from -0.0625 to 0.0625
- kernel_map: int32 [8, 4, 27, 384], P('space', 'fsdp'), may hold values from 0 to 1536, as said below
- counts: int32 [8, 4, 3], P('space', 'fsdp'), may hold values from 1 to 128, as said below
- halo_list: int32 [8, 4, 1], P('space', 'fsdp'), may hold values from 0 to 2
- skip_dest: int32 [8, 4, 384, 1], P('space', 'fsdp'), may hold values from 0 to 7; in each aligned block of 384 rows (0 to 383, 384 to 767, ..., all dimensions but the last counted through in order) at most 96 rows name the same one
- out_grad: bfloat16 [8, 4, 384, 384], P('space', 'fsdp'), may hold values from -6 to 6
Outputs:
- section_out: bfloat16 [8, 4, 384, 384], P('space', 'fsdp')
- feature_grad: bfloat16 [8, 4, 384, 384], P('space', 'fsdp')
- skip_recv: bfloat16 [8, 4, 8, 96, 384], P('space', 'fsdp')
Inputs may be any that keep to these rules, and one draw needn't show every extreme that they name: kernel_map[s, f, k, i] is a row of the table lookup[s, f]; the value 1536 means that offset k has no neighbour; at the middle offset every row names itself. `counts`: every device has a block with all 128 slots active. `skip_dest`: at most 96 rows of one device name one owner, and in every draw some device sends exactly 96 rows to some owner.
All inputs are finite; a program needn't handle non-finite values.
Results may differ from a plain program's by a relative error of at most 0.0045.
Values may be sent and summed in bfloat16 or wider, within the bound.
A program may use at most 64 MiB of HBM per device.

v0:
```python
import jax
import jax.numpy as jnp
from jax import lax
from jax.sharding import PartitionSpec as P

BLK = 128
KOFF = 27
HB = 1
NB = 3
ROWS = 1536


NORM_EPS = 1e-06


def padded(cells, sides, width):
    for axis, dim in sides:
        count = lax.axis_size(axis)
        ends = count - 1
        head = lax.slice_in_dim(cells, 0, width, axis=dim)
        tail = lax.slice_in_dim(cells, cells.shape[dim] - width, cells.shape[dim], axis=dim)
        cells = jnp.concatenate(
            [
                lax.ppermute(tail, axis, [(i, (i + 1) % count) for i in range(ends)]),
                cells,
                lax.ppermute(head, axis, [((i + 1) % count, i) for i in range(ends)]),
            ],
            axis=dim,
        )
    return cells


def passed_along(x, axis, by):
    count = lax.axis_size(axis)
    pairs = [(i, i + by) for i in range(count) if 0 <= i + by < count]
    return lax.ppermute(x, axis, pairs)


def shards(features, channel_gain, conv_weight, kernel_map, counts, halo_list, skip_dest, out_grad):
    own_rows = features[0, 0]
    rowcount = own_rows.shape[0]
    width = own_rows.shape[1]
    slot_ids = jnp.arange(rowcount, dtype=jnp.int32)
    limits = jnp.repeat(counts[0, 0], BLK)
    active = (slot_ids % BLK < limits).astype(jnp.float32)[:, None]
    masked = own_rows * active.astype(jnp.bfloat16)
    masked_f = masked.astype(jnp.float32)
    rscale = lax.rsqrt(jnp.mean(masked_f * masked_f, axis=-1, keepdims=True) + NORM_EPS)
    normed = masked_f * rscale
    pre_act = normed * channel_gain
    act = jax.nn.silu(pre_act).astype(jnp.bfloat16)
    shared = act.reshape(NB, BLK, width)[halo_list[0, 0]]
    beside_all = padded(shared[None, None], (("space", 0), ("fsdp", 1)), 1)
    lookup = jnp.concatenate(
        [act, beside_all.reshape(9 * HB * BLK, width), jnp.zeros((1, width), jnp.bfloat16)], axis=0
    )
    row_grad = out_grad[0, 0] * active.astype(jnp.bfloat16)
    groups = KOFF // 3
    weight_groups = conv_weight.reshape(groups, 3, conv_weight.shape[1], conv_weight.shape[2])
    map_groups = kernel_map[0, 0].reshape(groups, 3, rowcount)

    def group_step(state, inputs_g):
        running, table_grad = state
        weight_piece, neighbours = inputs_g
        widened = lax.all_gather(weight_piece, "fsdp", axis=2, tiled=True)
        full_weights = lax.all_gather(widened, "space", axis=1, tiled=True)
        picked = lookup[neighbours]
        running = running + jnp.einsum(
            "kvc,kcd->vd", picked, full_weights, preferred_element_type=jnp.float32
        )
        backward = jnp.einsum(
            "vd,kcd->kvc", row_grad, full_weights, preferred_element_type=jnp.float32
        )
        table_grad = table_grad.at[neighbours.reshape(-1)].add(backward.reshape(-1, width))
        return ((running, table_grad), None)

    start = (jnp.zeros((rowcount, width), jnp.float32), jnp.zeros((ROWS + 1, width), jnp.float32))
    (conv_sum, table_grad), _ = lax.scan(group_step, start, (weight_groups, map_groups))
    section_out = ((masked_f + conv_sum) * active).astype(jnp.bfloat16)
    owners = skip_dest[0, 0, :, 0]
    earlier = (owners[None, :] == owners[:, None]) & (slot_ids[None, :] < slot_ids[:, None])
    placing = jnp.sum(earlier.astype(jnp.int32), axis=1)
    space_size = lax.axis_size("space")
    capacity = max(2, 2 * rowcount // space_size)
    outbox = (
        jnp.zeros((space_size * capacity, width), jnp.bfloat16)
        .at[owners * capacity + placing]
        .set(section_out)
    )
    received = lax.all_to_all(
        outbox.reshape(space_size, capacity, width),
        "space",
        split_axis=0,
        concat_axis=0,
        tiled=True,
    )
    halo_grad = table_grad[rowcount : rowcount + 9 * HB * BLK].reshape(3, 3, HB, BLK, width)
    middle = halo_grad[1]
    for direction in (1, -1):
        middle = middle + passed_along(
            halo_grad[1 + direction].astype(jnp.bfloat16), "space", direction
        ).astype(jnp.float32)
    returned = middle[1]
    for direction in (1, -1):
        returned = returned + passed_along(
            middle[1 + direction].astype(jnp.bfloat16), "fsdp", direction
        ).astype(jnp.float32)
    act_grad = table_grad[:rowcount].reshape(NB, BLK, width).at[halo_list[0, 0]].add(returned)
    act_grad = act_grad.reshape(rowcount, width)
    sigmoid_pre = jax.nn.sigmoid(pre_act)
    pre_grad = act_grad * sigmoid_pre * (1.0 + pre_act * (1.0 - sigmoid_pre))
    normed_grad = pre_grad * channel_gain
    masked_grad = rscale * (
        normed_grad - normed * jnp.mean(normed_grad * normed, axis=-1, keepdims=True)
    )
    feature_grad = ((row_grad.astype(jnp.float32) + masked_grad) * active).astype(jnp.bfloat16)
    return (section_out[None, None], feature_grad[None, None], received[None, None])


def solution(mesh):
    return jax.shard_map(
        shards,
        mesh=mesh,
        in_specs=(
            P("space", "fsdp", None, None),
            P(),
            P(None, "space", "fsdp"),
            P("space", "fsdp", None, None),
            P("space", "fsdp", None),
            P("space", "fsdp", None),
            P("space", "fsdp", None, None),
            P("space", "fsdp", None, None),
        ),
        out_specs=(
            P("space", "fsdp", None, None),
            P("space", "fsdp", None, None),
            P("space", "fsdp", None, None, None),
        ),
        check_vma=False,
    )
```

profile of v0, /device:TPU:13, one launch (start us, length us, event | category | flops | bytes accessed | tf_op | source)
XLA Modules:
  0.0 628.6 jit_solution(11238118842914617021)
XLA Ops:
  6.0 2.1 collective-permute-start.1
  8.1 4.0 collective-permute-start
  13.3 2.0 collective-permute-done
  15.3 2.8 collective-permute-start.3
  18.1 3.0 collective-permute-start.2
  26.4 563.1 %while.15 = (s32[]{:T(128)}, f32[384,384]{1,0:T(8,128)}, f32[1537,384]{1,0:T(8,128)S(1)}, s32[9,3,384]{2,1,0:T(4,128)S(1)}, bf16[1537,384]{1,0:T(8,128)(2,1)}, /...) while((s32[]{:T(128)}, f32[384,384]{1,0:T(8,128)}, ...), condition=%wide.region_3.4_spmd.clone, body=%wide.region_1.3_spmd.clone.sunk | while | flops 680223488 | bytes 16021199 | solution.py:78
  26.5 5.8 gather_fusion
  33.2 7.7 %all-gather.6 = bf16[1,3,48,384]{2,1,0,3:T(4,128)(2,1)S(1)} all-gather(bf16[1,3,48,96]{2,1,0,3:T(4,128)(2,1)S(1)} %copy.38), channel_id=2, replica_groups=mesh['space'=8,'fsdp'=4] {'fsdp'}, dimensions={3}, use_global_device_ids=true | all-gather | bytes 138240 | tf_op jit(solution)/shard_map/while/body/eval_jaxpr/all_gather | solution.py:65
  41.7 25.5 %all-gather.7 = bf16[1,3,384,384]{3,2,1,0:T(8,128)(2,1)S(1)} all-gather(bf16[1,3,48,384]{3,2,1,0:T(8,128)(2,1)} %copy.39), channel_id=3, replica_groups=mesh['space'=8,'fsdp'=4] {'space'}, dimensions={2}, use_global_device_ids=true | all-gather | bytes 995328 | tf_op jit(solution)/shard_map/while/body/eval_jaxpr/all_gather | solution.py:66
  67.2 2.7 fusion.55
  71.2 1.9 fusion.57
  73.2 11.0 %scatter_fusion = f32[1537,384]{1,0:T(8,128)S(1)} fusion(f32[1537,384]{1,0:T(8,128)S(1)} %get-tuple-element.186, s32[1152]{0:T(1024)} %fusion.56, f32[1152,384]{1,0:T(8,128)} %bitcast.110), kind=kCustom, calls=%fused_computation.1.clone.clone.1 | custom fusion | flops 442368 | bytes 5313024 | tf_op jit(solution)/shard_map/while/body/eval_jaxpr/scatter-add | solution.py:74
  84.2 5.8 gather_fusion
  90.9 10.3 %all-gather.6 = bf16[1,3,48,384]{2,1,0,3:T(4,128)(2,1)S(1)} all-gather(bf16[1,3,48,96]{2,1,0,3:T(4,128)(2,1)S(1)} %copy.38), channel_id=2, replica_groups=mesh['space'=8,'fsdp'=4] {'fsdp'}, dimensions={3}, use_global_device_ids=true | all-gather | bytes 138240 | tf_op jit(solution)/shard_map/while/body/eval_jaxpr/all_gather | solution.py:65
  102.0 27.0 %all-gather.7 = bf16[1,3,384,384]{3,2,1,0:T(8,128)(2,1)S(1)} all-gather(bf16[1,3,48,384]{3,2,1,0:T(8,128)(2,1)} %copy.39), channel_id=3, replica_groups=mesh['space'=8,'fsdp'=4] {'space'}, dimensions={2}, use_global_device_ids=true | all-gather | bytes 995328 | tf_op jit(solution)/shard_map/while/body/eval_jaxpr/all_gather | solution.py:66
  129.0 2.8 fusion.55
  135.1 11.0 %scatter_fusion = f32[1537,384]{1,0:T(8,128)S(1)} fusion(f32[1537,384]{1,0:T(8,128)S(1)} %get-tuple-element.186, s32[1152]{0:T(1024)} %fusion.56, f32[1152,384]{1,0:T(8,128)} %bitcast.110), kind=kCustom, calls=%fused_computation.1.clone.clone.1 | custom fusion | flops 442368 | bytes 5313024 | tf_op jit(solution)/shard_map/while/body/eval_jaxpr/scatter-add | solution.py:74
  146.2 5.8 gather_fusion
  152.9 11.6 %all-gather.6 = bf16[1,3,48,384]{2,1,0,3:T(4,128)(2,1)S(1)} all-gather(bf16[1,3,48,96]{2,1,0,3:T(4,128)(2,1)S(1)} %copy.38), channel_id=2, replica_groups=mesh['space'=8,'fsdp'=4] {'fsdp'}, dimensions={3}, use_global_device_ids=true | all-gather | bytes 138240 | tf_op jit(solution)/shard_map/while/body/eval_jaxpr/all_gather | solution.py:65
  165.4 26.7 %all-gather.7 = bf16[1,3,384,384]{3,2,1,0:T(8,128)(2,1)S(1)} all-gather(bf16[1,3,48,384]{3,2,1,0:T(8,128)(2,1)} %copy.39), channel_id=3, replica_groups=mesh['space'=8,'fsdp'=4] {'space'}, dimensions={2}, use_global_device_ids=true | all-gather | bytes 995328 | tf_op jit(solution)/shard_map/while/body/eval_jaxpr/all_gather | solution.py:66
  192.1 2.8 fusion.55
  196.2 1.9 fusion.57
  198.1 11.0 %scatter_fusion = f32[1537,384]{1,0:T(8,128)S(1)} fusion(f32[1537,384]{1,0:T(8,128)S(1)} %get-tuple-element.186, s32[1152]{0:T(1024)} %fusion.56, f32[1152,384]{1,0:T(8,128)} %bitcast.110), kind=kCustom, calls=%fused_computation.1.clone.clone.1 | custom fusion | flops 442368 | bytes 5313024 | tf_op jit(solution)/shard_map/while/body/eval_jaxpr/scatter-add | solution.py:74
  209.2 5.8 gather_fusion
  215.9 12.0 %all-gather.6 = bf16[1,3,48,384]{2,1,0,3:T(4,128)(2,1)S(1)} all-gather(bf16[1,3,48,96]{2,1,0,3:T(4,128)(2,1)S(1)} %copy.38), channel_id=2, replica_groups=mesh['space'=8,'fsdp'=4] {'fsdp'}, dimensions={3}, use_global_device_ids=true | all-gather | bytes 138240 | tf_op jit(solution)/shard_map/while/body/eval_jaxpr/all_gather | solution.py:65
  228.7 27.0 %all-gather.7 = bf16[1,3,384,384]{3,2,1,0:T(8,128)(2,1)S(1)} all-gather(bf16[1,3,48,384]{3,2,1,0:T(8,128)(2,1)} %copy.39), channel_id=3, replica_groups=mesh['space'=8,'fsdp'=4] {'space'}, dimensions={2}, use_global_device_ids=true | all-gather | bytes 995328 | tf_op jit(solution)/shard_map/while/body/eval_jaxpr/all_gather | solution.py:66
  255.7 2.8 fusion.55
  259.9 1.9 fusion.57
  261.8 11.0 %scatter_fusion = f32[1537,384]{1,0:T(8,128)S(1)} fusion(f32[1537,384]{1,0:T(8,128)S(1)} %get-tuple-element.186, s32[1152]{0:T(1024)} %fusion.56, f32[1152,384]{1,0:T(8,128)} %bitcast.110), kind=kCustom, calls=%fused_computation.1.clone.clone.1 | custom fusion | flops 442368 | bytes 5313024 | tf_op jit(solution)/shard_map/while/body/eval_jaxpr/scatter-add | solution.py:74
  272.8 5.8 gather_fusion
  279.5 11.8 %all-gather.6 = bf16[1,3,48,384]{2,1,0,3:T(4,128)(2,1)S(1)} all-gather(bf16[1,3,48,96]{2,1,0,3:T(4,128)(2,1)S(1)} %copy.38), channel_id=2, replica_groups=mesh['space'=8,'fsdp'=4] {'fsdp'}, dimensions={3}, use_global_device_ids=true | all-gather | bytes 138240 | tf_op jit(solution)/shard_map/while/body/eval_jaxpr/all_gather | solution.py:65
  292.1 26.8 %all-gather.7 = bf16[1,3,384,384]{3,2,1,0:T(8,128)(2,1)S(1)} all-gather(bf16[1,3,48,384]{3,2,1,0:T(8,128)(2,1)} %copy.39), channel_id=3, replica_groups=mesh['space'=8,'fsdp'=4] {'space'}, dimensions={2}, use_global_device_ids=true | all-gather | bytes 995328 | tf_op jit(solution)/shard_map/while/body/eval_jaxpr/all_gather | solution.py:66
  318.9 2.8 fusion.55
  323.1 1.9 fusion.57
  325.0 11.0 %scatter_fusion = f32[1537,384]{1,0:T(8,128)S(1)} fusion(f32[1537,384]{1,0:T(8,128)S(1)} %get-tuple-element.186, s32[1152]{0:T(1024)} %fusion.56, f32[1152,384]{1,0:T(8,128)} %bitcast.110), kind=kCustom, calls=%fused_computation.1.clone.clone.1 | custom fusion | flops 442368 | bytes 5313024 | tf_op jit(solution)/shard_map/while/body/eval_jaxpr/scatter-add | solution.py:74
  336.1 5.8 gather_fusion
  342.7 11.9 %all-gather.6 = bf16[1,3,48,384]{2,1,0,3:T(4,128)(2,1)S(1)} all-gather(bf16[1,3,48,96]{2,1,0,3:T(4,128)(2,1)S(1)} %copy.38), channel_id=2, replica_groups=mesh['space'=8,'fsdp'=4] {'fsdp'}, dimensions={3}, use_global_device_ids=true | all-gather | bytes 138240 | tf_op jit(solution)/shard_map/while/body/eval_jaxpr/all_gather | solution.py:65
  355.5 26.7 %all-gather.7 = bf16[1,3,384,384]{3,2,1,0:T(8,128)(2,1)S(1)} all-gather(bf16[1,3,48,384]{3,2,1,0:T(8,128)(2,1)} %copy.39), channel_id=3, replica_groups=mesh['space'=8,'fsdp'=4] {'space'}, dimensions={2}, use_global_device_ids=true | all-gather | bytes 995328 | tf_op jit(solution)/shard_map/while/body/eval_jaxpr/all_gather | solution.py:66
  382.2 2.8 fusion.55
  388.3 11.0 %scatter_fusion = f32[1537,384]{1,0:T(8,128)S(1)} fusion(f32[1537,384]{1,0:T(8,128)S(1)} %get-tuple-element.186, s32[1152]{0:T(1024)} %fusion.56, f32[1152,384]{1,0:T(8,128)} %bitcast.110), kind=kCustom, calls=%fused_computation.1.clone.clone.1 | custom fusion | flops 442368 | bytes 5313024 | tf_op jit(solution)/shard_map/while/body/eval_jaxpr/scatter-add | solution.py:74
  399.3 5.8 gather_fusion
  406.0 12.0 %all-gather.6 = bf16[1,3,48,384]{2,1,0,3:T(4,128)(2,1)S(1)} all-gather(bf16[1,3,48,96]{2,1,0,3:T(4,128)(2,1)S(1)} %copy.38), channel_id=2, replica_groups=mesh['space'=8,'fsdp'=4] {'fsdp'}, dimensions={3}, use_global_device_ids=true | all-gather | bytes 138240 | tf_op jit(solution)/shard_map/while/body/eval_jaxpr/all_gather | solution.py:65
  418.9 26.8 %all-gather.7 = bf16[1,3,384,384]{3,2,1,0:T(8,128)(2,1)S(1)} all-gather(bf16[1,3,48,384]{3,2,1,0:T(8,128)(2,1)} %copy.39), channel_id=3, replica_groups=mesh['space'=8,'fsdp'=4] {'space'}, dimensions={2}, use_global_device_ids=true | all-gather | bytes 995328 | tf_op jit(solution)/shard_map/while/body/eval_jaxpr/all_gather | solution.py:66
  445.7 2.8 fusion.55
  449.9 1.9 fusion.57
  451.8 11.0 %scatter_fusion = f32[1537,384]{1,0:T(8,128)S(1)} fusion(f32[1537,384]{1,0:T(8,128)S(1)} %get-tuple-element.186, s32[1152]{0:T(1024)} %fusion.56, f32[1152,384]{1,0:T(8,128)} %bitcast.110), kind=kCustom, calls=%fused_computation.1.clone.clone.1 | custom fusion | flops 442368 | bytes 5313024 | tf_op jit(solution)/shard_map/while/body/eval_jaxpr/scatter-add | solution.py:74
  462.8 5.8 gather_fusion
  469.5 11.9 %all-gather.6 = bf16[1,3,48,384]{2,1,0,3:T(4,128)(2,1)S(1)} all-gather(bf16[1,3,48,96]{2,1,0,3:T(4,128)(2,1)S(1)} %copy.38), channel_id=2, replica_groups=mesh['space'=8,'fsdp'=4] {'fsdp'}, dimensions={3}, use_global_device_ids=true | all-gather | bytes 138240 | tf_op jit(solution)/shard_map/while/body/eval_jaxpr/all_gather | solution.py:65
  482.3 27.0 %all-gather.7 = bf16[1,3,384,384]{3,2,1,0:T(8,128)(2,1)S(1)} all-gather(bf16[1,3,48,384]{3,2,1,0:T(8,128)(2,1)} %copy.39), channel_id=3, replica_groups=mesh['space'=8,'fsdp'=4] {'space'}, dimensions={2}, use_global_device_ids=true | all-gather | bytes 995328 | tf_op jit(solution)/shard_map/while/body/eval_jaxpr/all_gather | solution.py:66
  509.2 2.8 fusion.55
  515.3 11.0 %scatter_fusion = f32[1537,384]{1,0:T(8,128)S(1)} fusion(f32[1537,384]{1,0:T(8,128)S(1)} %get-tuple-element.186, s32[1152]{0:T(1024)} %fusion.56, f32[1152,384]{1,0:T(8,128)} %bitcast.110), kind=kCustom, calls=%fused_computation.1.clone.clone.1 | custom fusion | flops 442368 | bytes 5313024 | tf_op jit(solution)/shard_map/while/body/eval_jaxpr/scatter-add | solution.py:74
  526.4 5.8 gather_fusion
  533.1 11.8 %all-gather.6 = bf16[1,3,48,384]{2,1,0,3:T(4,128)(2,1)S(1)} all-gather(bf16[1,3,48,96]{2,1,0,3:T(4,128)(2,1)S(1)} %copy.38), channel_id=2, replica_groups=mesh['space'=8,'fsdp'=4] {'fsdp'}, dimensions={3}, use_global_device_ids=true | all-gather | bytes 138240 | tf_op jit(solution)/shard_map/while/body/eval_jaxpr/all_gather | solution.py:65
  545.7 26.8 %all-gather.7 = bf16[1,3,384,384]{3,2,1,0:T(8,128)(2,1)S(1)} all-gather(bf16[1,3,48,384]{3,2,1,0:T(8,128)(2,1)} %copy.39), channel_id=3, replica_groups=mesh['space'=8,'fsdp'=4] {'space'}, dimensions={2}, use_global_device_ids=true | all-gather | bytes 995328 | tf_op jit(solution)/shard_map/while/body/eval_jaxpr/all_gather | solution.py:66
  572.5 2.8 fusion.55
  576.6 1.9 fusion.57
  578.5 11.0 %scatter_fusion = f32[1537,384]{1,0:T(8,128)S(1)} fusion(f32[1537,384]{1,0:T(8,128)S(1)} %get-tuple-element.186, s32[1152]{0:T(1024)} %fusion.56, f32[1152,384]{1,0:T(8,128)} %bitcast.110), kind=kCustom, calls=%fused_computation.1.clone.clone.1 | custom fusion | flops 442368 | bytes 5313024 | tf_op jit(solution)/shard_map/while/body/eval_jaxpr/scatter-add | solution.py:74
  590.6 3.5 collective-permute-start.5
  594.1 2.6 collective-permute-start.4
  597.6 3.0 scatter_custom_fusion.1
  600.6 8.2 %all-to-all-start = ((bf16[8,96,384]{2,1,0:T(8,128)(2,1)}), bf16[8,96,384]{2,1,0:T(8,128)(2,1)}, u32[]{:S(2)}, u32[]{:S(2)}) async-start(bf16[8,96,384]{2,1,0:T(8,128)(2,1)} %bitcast.117), calls=%async_computation | async-start | bytes 1179648 | tf_op jit(solution)/shard_map/all_to_all | solution.py:90
  610.9 8.9 %collective-permute-start.7 = (bf16[1,128,384]{2,1,0:T(8,128)(2,1)S(1)}, bf16[1,128,384]{2,1,0:T(8,128)(2,1)S(1)}, u32[]{:S(2)}, u32[]{:S(2)}) collective-permute-start(bf16[1,128,384]{2,1,0:T(8,128)(2,1)S(1)} %get-tuple-element.129), channel_id=1, source_target_pairs={{1,0},{2,1},{3,2},{5,4},{6,5},{7,6},{9,8},{10,9},{11,10},{13,12},{... | collective-permute-start | bytes 294920 | tf_op jit(solution)/shard_map/ppermute | solution.py:36
  619.8 2.7 collective-permute-start.6
  626.7 1.9 copy.54
  (210 shorter events, 52.5 us)
Async XLA Ops:
  0.6 21.3 %copy-start.1 = (bf16[1,1,384,384]{3,2,1,0:T(8,128)(2,1)S(1)}, bf16[1,1,384,384]{3,2,1,0:T(8,128)(2,1)}, u32[]{:S(2)}) copy-start(bf16[1,1,384,384]{3,2,1,0:T(8,128)(2,1)} %param.12) | copy-start | bytes 884740
  0.6 21.3 %copy-start.9 = (f32[384]{0:T(512)S(1)}, f32[384]{0:T(512)}, u32[]{:S(2)}) copy-start(f32[384]{0:T(512)} %param.13) | copy-start | bytes 4612
  0.7 11.5 %copy-start.3 = (bf16[1,1,384,384]{3,2,1,0:T(8,128)(2,1)S(1)}, bf16[1,1,384,384]{3,2,1,0:T(8,128)(2,1)}, u32[]{:S(2)}) copy-start(bf16[1,1,384,384]{3,2,1,0:T(8,128)(2,1)} %param.19) | copy-start | bytes 884740
  0.7 12.3 %copy-start.16 = (s32[1,1,384,1]{2,3,1,0:T(1,128)S(1)}, s32[1,1,384,1]{2,3,1,0:T(1,128)}, u32[]{:S(2)}) copy-start(s32[1,1,384,1]{2,3,1,0:T(1,128)} %param.18) | copy-start | bytes 4612
  0.7 21.1 %copy-start.8 = (s32[1,1,27,384]{3,1,2,0:T(1,128)S(1)}, s32[1,1,27,384]{3,1,2,0:T(1,128)}, u32[]{:S(2)}) copy-start(s32[1,1,27,384]{3,1,2,0:T(1,128)} %param.15) | copy-start | bytes 124420
  2.8 10.2 %copy-start.17 = (bf16[3,128]{1,0:T(4,128)(2,1)}, bf16[3,128]{1,0:T(4,128)(2,1)S(1)}, u32[]{:S(2)}) copy-start(bf16[3,128]{1,0:T(4,128)(2,1)S(1)} %convert_convert_fusion) | copy-start | bytes 2308
  4.0 20.9 %copy-start.12 = (f32[384]{0:T(512)}, f32[384]{0:T(512)S(1)}, u32[]{:S(2)}) copy-start(f32[384]{0:T(512)S(1)} %get-tuple-element.130) | copy-start | bytes 4612
  4.0 20.9 %copy-start.14 = (f32[3,128]{1,0:T(4,128)}, f32[3,128]{1,0:T(4,128)S(1)}, u32[]{:S(2)}) copy-start(f32[3,128]{1,0:T(4,128)S(1)} %get-tuple-element.131) | copy-start | bytes 4612
  6.0 7.3 %collective-permute-start.1 = (bf16[1,1,1,128,384]{4,3,1,0,2:T(8,128)(2,1)S(1)}, bf16[1,1,1,128,384]{4,3,1,0,2:T(8,128)(2,1)S(1)}, u32[]{:S(2)}, u32[]{:S(2)}) collective-permute-start(bf16[1,1,1,128,384]{4,3,1,0,2:T(8,128)(2,1)S(1)} %fusion.24), channel_id=1, source_target_pairs={{4,0},{8,4},{12,8},{16,12},{20,16},{24,20},{28,24},{5,1},{9,5},{13... | collective-permute-start | bytes 294920 | tf_op jit(solution)/shard_map/ppermute | solution.py:26
  8.1 7.2 %collective-permute-start = (bf16[1,1,1,128,384]{4,3,1,0,2:T(8,128)(2,1)S(1)}, bf16[1,1,1,128,384]{4,3,1,0,2:T(8,128)(2,1)S(1)}, u32[]{:S(2)}, u32[]{:S(2)}) collective-permute-start(bf16[1,1,1,128,384]{4,3,1,0,2:T(8,128)(2,1)S(1)} %fusion.24), channel_id=1, source_target_pairs={{0,4},{4,8},{8,12},{12,16},{16,20},{20,24},{24,28},{1,5},{5,9},{9,... | collective-permute-start | bytes 294920 | tf_op jit(solution)/shard_map/ppermute | solution.py:24
  15.3 8.3 %collective-permute-start.3 = (bf16[3,1,1,128,384]{4,3,1,0,2:T(8,128)(2,1)S(1)}, bf16[3,1,1,128,384]{4,3,1,0,2:T(8,128)(2,1)S(1)}, u32[]{:S(2)}, u32[]{:S(2)}) collective-permute-start(bf16[3,1,1,128,384]{4,3,1,0,2:T(8,128)(2,1)S(1)} %pad_maximum_fusion.1), channel_id=1, source_target_pairs={{1,0},{2,1},{3,2},{5,4},{6,5},{7,6},{9,8},{10,9},{11,10},{13,12},{... | collective-permute-start | bytes 884744 | tf_op jit(solution)/shard_map/ppermute | solution.py:26
  18.1 6.7 %collective-permute-start.2 = (bf16[3,1,1,128,384]{4,3,1,0,2:T(8,128)(2,1)S(1)}, bf16[3,1,1,128,384]{4,3,1,0,2:T(8,128)(2,1)S(1)}, u32[]{:S(2)}, u32[]{:S(2)}) collective-permute-start(bf16[3,1,1,128,384]{4,3,1,0,2:T(8,128)(2,1)S(1)} %pad_maximum_fusion.1), channel_id=1, source_target_pairs={{0,1},{1,2},{2,3},{4,5},{5,6},{6,7},{8,9},{9,10},{10,11},{12,13},{... | collective-permute-start | bytes 884744 | tf_op jit(solution)/shard_map/ppermute | solution.py:24
  26.4 5.8 copy-start.6
  67.2 4.0 copy-start.2
  73.1 11.0 %copy-start.7 = (s32[9,3,384]{2,1,0:T(4,128)S(1)}, s32[9,3,384]{2,1,0:T(4,128)}, u32[]{:S(2)}) copy-start(s32[9,3,384]{2,1,0:T(4,128)} %copy-done.6) | copy-start | bytes 124420 | tf_op jit(solution)/shard_map/while
  84.2 5.8 copy-start.6
  129.0 4.2 copy-start.2
  135.1 11.0 %copy-start.7 = (s32[9,3,384]{2,1,0:T(4,128)S(1)}, s32[9,3,384]{2,1,0:T(4,128)}, u32[]{:S(2)}) copy-start(s32[9,3,384]{2,1,0:T(4,128)} %copy-done.6) | copy-start | bytes 124420 | tf_op jit(solution)/shard_map/while
  146.1 5.8 copy-start.6
  192.1 4.2 copy-start.2
  198.1 11.0 %copy-start.7 = (s32[9,3,384]{2,1,0:T(4,128)S(1)}, s32[9,3,384]{2,1,0:T(4,128)}, u32[]{:S(2)}) copy-start(s32[9,3,384]{2,1,0:T(4,128)} %copy-done.6) | copy-start | bytes 124420 | tf_op jit(solution)/shard_map/while
  209.1 5.8 copy-start.6
  255.7 4.2 copy-start.2
  261.8 11.0 %copy-start.7 = (s32[9,3,384]{2,1,0:T(4,128)S(1)}, s32[9,3,384]{2,1,0:T(4,128)}, u32[]{:S(2)}) copy-start(s32[9,3,384]{2,1,0:T(4,128)} %copy-done.6) | copy-start | bytes 124420 | tf_op jit(solution)/shard_map/while
  272.8 5.8 copy-start.6
  318.9 4.2 copy-start.2
  325.0 11.0 %copy-start.7 = (s32[9,3,384]{2,1,0:T(4,128)S(1)}, s32[9,3,384]{2,1,0:T(4,128)}, u32[]{:S(2)}) copy-start(s32[9,3,384]{2,1,0:T(4,128)} %copy-done.6) | copy-start | bytes 124420 | tf_op jit(solution)/shard_map/while
  336.0 5.8 copy-start.6
  382.2 4.2 copy-start.2
  388.2 11.0 %copy-start.7 = (s32[9,3,384]{2,1,0:T(4,128)S(1)}, s32[9,3,384]{2,1,0:T(4,128)}, u32[]{:S(2)}) copy-start(s32[9,3,384]{2,1,0:T(4,128)} %copy-done.6) | copy-start | bytes 124420 | tf_op jit(solution)/shard_map/while
  399.3 5.8 copy-start.6
  445.7 4.2 copy-start.2
  451.8 11.0 %copy-start.7 = (s32[9,3,384]{2,1,0:T(4,128)S(1)}, s32[9,3,384]{2,1,0:T(4,128)}, u32[]{:S(2)}) copy-start(s32[9,3,384]{2,1,0:T(4,128)} %copy-done.6) | copy-start | bytes 124420 | tf_op jit(solution)/shard_map/while
  462.8 5.8 copy-start.6
  509.2 4.2 copy-start.2
  515.3 11.0 %copy-start.7 = (s32[9,3,384]{2,1,0:T(4,128)S(1)}, s32[9,3,384]{2,1,0:T(4,128)}, u32[]{:S(2)}) copy-start(s32[9,3,384]{2,1,0:T(4,128)} %copy-done.6) | copy-start | bytes 124420 | tf_op jit(solution)/shard_map/while
  526.3 5.8 copy-start.6
  572.5 4.2 copy-start.2
  578.5 11.0 %copy-start.7 = (s32[9,3,384]{2,1,0:T(4,128)S(1)}, s32[9,3,384]{2,1,0:T(4,128)}, u32[]{:S(2)}) copy-start(s32[9,3,384]{2,1,0:T(4,128)} %copy-done.6) | copy-start | bytes 124420 | tf_op jit(solution)/shard_map/while
  589.5 7.2 %copy-start.19 = (s32[3]{0:T(128)S(1)}, s32[3]{0:T(128)}, u32[]{:S(2)}) copy-start(s32[3]{0:T(128)} %constant.76.clone.1) | copy-start | bytes 40
  589.6 8.0 %copy-start = (f32[384,384]{1,0:T(8,128)S(1)}, f32[384,384]{1,0:T(8,128)}, u32[]{:S(2)}) copy-start(f32[384,384]{1,0:T(8,128)} %get-tuple-element.53) | copy-start | bytes 1769476
  590.6 18.4 %collective-permute-start.5 = (bf16[3,1,128,384]{3,2,1,0:T(8,128)(2,1)}, bf16[3,1,128,384]{3,2,1,0:T(8,128)(2,1)S(1)}, u32[]{:S(2)}, u32[]{:S(2)}) collective-permute-start(bf16[3,1,128,384]{3,2,1,0:T(8,128)(2,1)} %bitcast.18), channel_id=1, source_target_pairs={{4,0},{8,4},{12,8},{16,12},{20,16},{24,20},{28,24},{5,1},{9,5},{13... | collective-permute-start | bytes 884744 | tf_op jit(solution)/shard_map/ppermute | solution.py:36
  594.1 14.8 %collective-permute-start.4 = (bf16[3,1,128,384]{3,2,1,0:T(8,128)(2,1)}, bf16[3,1,128,384]{3,2,1,0:T(8,128)(2,1)}, u32[]{:S(2)}, u32[]{:S(2)}) collective-permute-start(bf16[3,1,128,384]{3,2,1,0:T(8,128)(2,1)} %bitcast.16), channel_id=1, source_target_pairs={{0,4},{4,8},{8,12},{12,16},{16,20},{20,24},{24,28},{1,5},{5,9},{9,... | collective-permute-start | bytes 884744 | tf_op jit(solution)/shard_map/ppermute | solution.py:36
  600.6 26.1 %all-to-all-start = ((bf16[8,96,384]{2,1,0:T(8,128)(2,1)}), bf16[8,96,384]{2,1,0:T(8,128)(2,1)}, u32[]{:S(2)}, u32[]{:S(2)}) async-start(bf16[8,96,384]{2,1,0:T(8,128)(2,1)} %bitcast.117), calls=%async_computation | async-start | bytes 1179648 | tf_op jit(solution)/shard_map/all_to_all | solution.py:90
  608.8 13.7 %copy-start.11 = (f32[384]{0:T(512)S(1)}, f32[384]{0:T(512)}, u32[]{:S(2)}) copy-start(f32[384]{0:T(512)} %get-tuple-element.121) | copy-start | bytes 4612
  608.9 16.0 %copy-start.10 = (f32[384]{0:T(512)S(1)}, f32[384]{0:T(512)}, u32[]{:S(2)}) copy-start(f32[384]{0:T(512)} %param.13) | copy-start | bytes 4612
  608.9 16.0 %copy-start.15 = (f32[3,128]{1,0:T(4,128)S(1)}, f32[3,128]{1,0:T(4,128)}, u32[]{:S(2)}) copy-start(f32[3,128]{1,0:T(4,128)} %copy-done.14) | copy-start | bytes 4612
  608.9 16.0 %copy-start.18 = (bf16[3,128]{1,0:T(4,128)(2,1)S(1)}, bf16[3,128]{1,0:T(4,128)(2,1)}, u32[]{:S(2)}) copy-start(bf16[3,128]{1,0:T(4,128)(2,1)} %copy-done.17) | copy-start | bytes 2308
  609.0 0.7 copy-start.5
  609.7 15.8 %copy-start.4 = (bf16[1,1,384,384]{3,2,1,0:T(8,128)(2,1)S(1)}, bf16[1,1,384,384]{3,2,1,0:T(8,128)(2,1)}, u32[]{:S(2)}) copy-start(bf16[1,1,384,384]{3,2,1,0:T(8,128)(2,1)} %param.19) | copy-start | bytes 884740
  609.7 15.8 %copy-start.13 = (f32[384]{0:T(512)S(1)}, f32[384]{0:T(512)}, u32[]{:S(2)}) copy-start(f32[384]{0:T(512)} %copy-done.12) | copy-start | bytes 4612
  610.9 12.5 %collective-permute-start.7 = (bf16[1,128,384]{2,1,0:T(8,128)(2,1)S(1)}, bf16[1,128,384]{2,1,0:T(8,128)(2,1)S(1)}, u32[]{:S(2)}, u32[]{:S(2)}) collective-permute-start(bf16[1,128,384]{2,1,0:T(8,128)(2,1)S(1)} %get-tuple-element.129), channel_id=1, source_target_pairs={{1,0},{2,1},{3,2},{5,4},{6,5},{7,6},{9,8},{10,9},{11,10},{13,12},{... | collective-permute-start | bytes 294920 | tf_op jit(solution)/shard_map/ppermute | solution.py:36
  619.8 4.3 collective-permute-start.6
where the time goes:
time: 632 us; the launch traced here: 629 us
  blocking collectives  341 us (54%)
  other arithmetic  121 us (19%)
  local copies, waits for them, and re-layouts  78.1 us (12%)
  matrix products  42.5 us (7%)
  starting transfers between devices  38 us (6%)
    all_gather x9, blocking collectives, group_step(): full_weights = lax.all_gather(widened, 'space', axis=1, tiled=True)  240 us
    all_gather x9, blocking collectives, group_step(): widened = lax.all_gather(weight_piece, 'fsdp', axis=2, tiled=True)  101 us
    scatter-add x9, other arithmetic, group_step(): table_grad.at[neighbours.reshape(-1)].add(backward.reshape(-1, width))  98.9 us
    gather x9, local copies, waits for them, and re-layouts, group_step(): picked = lookup[neighbours]  52 us
    dot_general x9, matrix products, group_step(): jnp.einsum('kvc,kcd->vd', picked, full_weights, preferred_element_type=jn...  25.4 us
    ppermute x4, starting transfers between devices, passed_along(): return lax.ppermute(x, axis, pairs)  17.8 us
    dot_general x9, matrix products, group_step(): jnp.einsum('vd,kcd->kvc', row_grad, full_weights, preferred_element_type=...  17.1 us
  transfers between devices with their start and end apart: 9, of which 4 were waited for; matrix products, arithmetic and copies ran while one was open for 2% of the time, Pallas kernels for 0%

commit v1 on v0

--- a/solution.py
+++ b/solution.py
@@ -1,6 +1,10 @@
+import functools
+
 import jax
 import jax.numpy as jnp
 from jax import lax
+from jax.experimental import pallas as pl
+from jax.experimental.pallas import tpu as pltpu
 from jax.sharding import PartitionSpec as P
 
 BLK = 128
@@ -36,7 +40,7 @@
     return lax.ppermute(x, axis, pairs)
 
 
-def shards(features, channel_gain, conv_weight, kernel_map, counts, halo_list, skip_dest, out_grad):
+def shards_plain(features, channel_gain, conv_weight, kernel_map, counts, halo_list, skip_dest, out_grad):
     own_rows = features[0, 0]
     rowcount = own_rows.shape[0]
     width = own_rows.shape[1]
@@ -117,9 +121,454 @@
     return (section_out[None, None], feature_grad[None, None], received[None, None])
 
 
+LANES = 128
+Q = 3
+MESH = pl.DeviceIdType.MESH
+F32 = jnp.float32
+BF16 = jnp.bfloat16
+
+
+def moved(x, shift):
+    shift = shift % LANES
+    return x if shift == 0 else pltpu.roll(x, shift, 1)
+
+
+def regroup(x, from_of, to_of, width, pieces):
+    lanes = lax.broadcasted_iota(jnp.int32, (x.shape[0], LANES), 1)
+    tiles = {}
+    for p in range(pieces):
+        r = 0
+        while r < width:
+            src, dst = from_of(p, r), to_of(p, r)
+            span = min(width - r, LANES - src % LANES, LANES - dst % LANES)
+            at = src // LANES * LANES
+            value = moved(x[:, at : at + LANES], dst - src)
+            low = dst % LANES
+            held = tiles.get(dst // LANES, jnp.zeros_like(value))
+            tiles[dst // LANES] = jnp.where((lanes >= low) & (lanes < low + span), value, held)
+            r += span
+    return jnp.concatenate([tiles[t] for t in range(len(tiles))], axis=1)
+
+
+def norm_parts(feat, active, gain):
+    masked = feat.astype(F32) * active
+    rscale = lax.rsqrt(jnp.mean(masked * masked, axis=-1, keepdims=True) + NORM_EPS)
+    normed = masked * rscale
+    return masked, rscale, normed, normed * gain
+
+
+def section_kernel(
+    dims, h_ref, feat, gain, active, og, wire, nmap, tgt,
+    sec, fgrad, recv,
+    wbuf, lookup, pb, conv, shared, rgp, w3, gsend, grecv, outbox,
+    wsend, wrecv, hsend, hrecv, ssend, srecv, bsend, brecv, own_sem,
+):
+    S, F, Z, G, K4 = dims
+    Y = 2
+    rows, C = feat.shape
+    width = C // F
+    table = lookup.shape[0]
+    s = lax.axis_index("space")
+    f = lax.axis_index("fsdp")
+    z, y = s // Y, s % Y
+    fx = (f + 2) % F
+    fp = f + 1 - 2 * (f % 2)
+    sy = s + 1 - 2 * y
+
+    def remote(src, dst, a, b, ss, ff):
+        return pltpu.make_async_remote_copy(
+            src_ref=src, dst_ref=dst, send_sem=a, recv_sem=b, device_id=(ss, ff), device_id_type=MESH
+        )
+
+    def inside(ds, df):
+        return (s + ds >= 0) & (s + ds < S) & (f + df >= 0) & (f + df < F)
+
+    around = [(ds, df) for ds in (-1, 0, 1) for df in (-1, 0, 1)]
+
+    own = pltpu.make_async_copy(wire, wbuf.at[:, f, :, z, y], own_sem)
+    own.start()
+    masked, rscale, normed, pre = norm_parts(feat[...], active[...], gain[...])
+    act = (pre / (1.0 + jnp.exp(-pre))).astype(BF16)
+    lookup[0:rows, :] = act
+    h = h_ref[0]
+    share = act[0:BLK]
+    for b in range(1, NB):
+        share = jnp.where(h == b, act[b * BLK : (b + 1) * BLK].astype(F32), share.astype(F32)).astype(BF16)
+    shared[...] = share
+    for n, (ds, df) in enumerate(around):
+        if ds == 0 and df == 0:
+            lookup[rows + n * BLK : rows + (n + 1) * BLK, :] = share
+        else:
+
+            @pl.when(jnp.logical_not(inside(ds, df)))
+            def _():
+                lookup[rows + n * BLK : rows + (n + 1) * BLK, :] = jnp.zeros((BLK, C), BF16)
+
+            @pl.when(jnp.logical_not(inside(-ds, -df)))
+            def _():
+                grecv[n] = jnp.zeros((BLK, C), BF16)
+
+    rg = (og[...].astype(F32) * active[...])
+    rgp[...] = regroup(
+        rg, lambda p, r: p * width + r, lambda p, r: p * LANES + r, width, F
+    ).astype(BF16)
+    conv[...] = jnp.zeros_like(conv)
+
+    barrier = pltpu.get_barrier_semaphore()
+    for d in range(1, S):
+        pl.semaphore_signal(barrier, inc=1, device_id=((s + d) % S, f), device_id_type=MESH)
+    for d in range(1, F):
+        pl.semaphore_signal(barrier, inc=1, device_id=(s, (f + d) % F), device_id_type=MESH)
+    for ds, df in around:
+        if ds and df:
+            pl.semaphore_signal(
+                barrier, inc=1, device_id=((s + ds + S) % S, (f + df + F) % F), device_id_type=MESH
+            )
+    pl.semaphore_wait(barrier, S + F - 2 + 4)
+
+    def halo(n, ds, df):
+        return remote(
+            shared, lookup.at[pl.ds(rows + n * BLK, BLK)], hsend.at[n], hrecv.at[n], s - ds, f - df
+        )
+
+    def first(g, d):
+        return remote(
+            wire.at[g], wbuf.at[g, f, :, z, y], wsend.at[g, d - 1], wrecv.at[g, d - 1],
+            ((z + d) % Z) * Y + y, f,
+        )
+
+    def strip(g, col, i, ss, ff):
+        ref = wbuf.at[g, col, :, :, y]
+        return remote(ref, ref, wsend.at[g, i], wrecv.at[g, i], ss, ff)
+
+    def column(g, col, i, ss, ff):
+        ref = wbuf.at[g, col]
+        return remote(ref, ref, wsend.at[g, i], wrecv.at[g, i], ss, ff)
+
+    B0 = Z - 1
+
+    def second_a(g):
+        return strip(g, f, B0, sy, f)
+
+    def second_b(g):
+        return strip(g, f, B0, s, fx)
+
+    def third_a(g):
+        return [column(g, f, B0 + 1, s, fx), column(g, f, B0 + 2, s, fp)]
+
+    def third_b(g):
+        return [strip(g, f, B0 + 1, sy, f), strip(g, fx, B0 + 4, sy, f)]
+
+    def fourth_a(g):
+        return [column(g, fx, B0 + 3, s, fp)]
+
+    def fourth_b(g):
+        return [column(g, f, B0 + 2, s, fp), column(g, fx, B0 + 3, s, fp)]
+
+    for n, (ds, df) in enumerate(around):
+        if ds or df:
+
+            @pl.when(inside(-ds, -df))
+            def _():
+                halo(n, ds, df).start()
+
+    @pl.loop(0, G)
+    def _(g):
+        for d in range(1, Z):
+            first(g, d).start()
+
+    own.wait()
+    for n, (ds, df) in enumerate(around):
+        if ds or df:
+
+            @pl.when(inside(ds, df))
+            def _():
+                halo(n, ds, df).wait_recv()
+
+    lane_u = lax.broadcasted_iota(jnp.int32, (rows, table), 1)
+
+    def gather(k):
+        line = jnp.broadcast_to(nmap[k], (8, rows))
+        ids = jnp.transpose(line)[:, 0:1]
+        pick = jnp.where(lane_u == ids, 1.0, 0.0).astype(BF16)
+        pb[k] = jnp.dot(pick, lookup[...], preferred_element_type=F32).astype(BF16)
+
+    def whole(g, j):
+        return jnp.concatenate([wbuf[g, p, j].reshape(C, LANES) for p in range(F)], axis=1)
+
+    def use(g, j, weights):
+        k = g * K4 + j
+        conv[...] += jnp.dot(pb[k], weights, preferred_element_type=F32)
+        pb[k] = lax.dot_general(
+            rgp[...], weights, (((1,), (1,)), ((), ())), preferred_element_type=F32
+        ).astype(BF16)
+
+    @pl.loop(0, G + 3)
+    def _(t):
+        @pl.when(t < G)
+        def _():
+            for d in range(1, Z):
+                first(t, d).wait_recv()
+
+            @pl.when(t % 2 == 0)
+            def _():
+                second_a(t).start()
+
+            @pl.when(t % 2 == 1)
+            def _():
+                second_b(t).start()
+
+        g3 = t - 1
+
+        @pl.when((g3 >= 0) & (g3 < G))
+        def _():
+            @pl.when(g3 % 2 == 0)
+            def _():
+                second_a(g3).wait_recv()
+                for c in third_a(g3):
+                    c.start()
+
+            @pl.when(g3 % 2 == 1)
+            def _():
+                second_b(g3).wait_recv()
+                for c in third_b(g3):
+                    c.start()
+
+        g4 = t - 2
+
+        @pl.when((g4 >= 0) & (g4 < G))
+        def _():
+            @pl.when(g4 % 2 == 0)
+            def _():
+                third_a(g4)[0].wait_recv()
+                for c in fourth_a(g4):
+                    c.start()
+
+            @pl.when(g4 % 2 == 1)
+            def _():
+                for c in third_b(g4):
+                    c.wait_recv()
+                for c in fourth_b(g4):
+                    c.start()
+
+        @pl.when(t < G)
+        def _():
+            @pl.loop(0, K4)
+            def _(j):
+                gather(t * K4 + j)
+
+        g5 = t - 3
+
+        @pl.when(g5 >= 0)
+        def _():
+            for c in fourth_b(g5):
+                c.wait_recv()
+            lanes = lax.broadcasted_iota(jnp.int32, (C, LANES), 1)
+            piece = LANES - width
+            for p in range(F):
+                tile = jnp.zeros((C, LANES), F32)
+                for q in range(Q):
+                    part = moved(wbuf[g5, p, q].reshape(C, LANES).astype(F32), q * piece - width)
+                    tile = jnp.where((lanes >= q * piece) & (lanes < (q + 1) * piece), part, tile)
+                w3[:, p * LANES : (p + 1) * LANES] = tile.astype(BF16)
+
+            @pl.loop(0, Q)
+            def _(j):
+                use(g5, j, whole(g5, j))
+
+            use(g5, Q, w3[...])
+
+    total = regroup(conv[...], lambda p, r: p * LANES + r, lambda p, r: p * width + r, width, F)
+    out = ((feat[...].astype(F32) * active[...] + total) * active[...]).astype(BF16)
+    sec[...] = out
+    cap = recv.shape[1]
+    slots = lax.broadcasted_iota(jnp.int32, (S * cap, rows), 0)
+    place = jnp.where(slots == tgt[...], 1.0, 0.0).astype(BF16)
+    outbox[...] = jnp.dot(place, out, preferred_element_type=F32).astype(BF16).reshape(S, cap, C)
+
+    def skip(d):
+        o = (s + d) % S
+        return remote(outbox.at[o], recv.at[s], ssend.at[d - 1], srecv.at[d - 1], o, f)
+
+    def scatter(u0):
+        def step(g, acc):
+            base = lax.broadcasted_iota(jnp.int32, (rows, rows), 0) + u0
+            hot = jnp.concatenate(
+                [jnp.where(base == nmap[g * K4 + j], 1.0, 0.0).astype(BF16) for j in range(K4)], axis=1
+            )
+            return acc + jnp.dot(
+                hot, pb[pl.ds(g * K4, K4)].reshape(K4 * rows, C), preferred_element_type=F32
+            )
+
+        return step
+
+    def grad(n, ds, df):
+        return remote(gsend.at[n], grecv.at[n], bsend.at[n], brecv.at[n], s + ds, f + df)
+
+    per = rows // BLK
+
+    def send_grads(c):
+        for n in range(c * per, (c + 1) * per):
+            ds, df = around[n]
+            if ds or df:
+
+                @pl.when(inside(ds, df))
+                def _():
+                    grad(n, ds, df).start()
+
+    keep = pltpu.make_async_copy(outbox.at[s], recv.at[s], own_sem)
+
+    @pl.loop(0, len(around) // per)
+    def _(c):
+        conv[:, 0:C] = jnp.zeros((rows, C), F32)
+
+        @pl.loop(0, G)
+        def _(g):
+            conv[:, 0:C] = scatter((c + 1) * rows)(g, conv[:, 0:C])
+
+        gsend[pl.ds(c * per, per)] = conv[:, 0:C].astype(BF16).reshape(per, BLK, C)
+
+        @pl.when(c == 0)
+        def _():
+            for d in range(1, S):
+                skip(d).start()
+            keep.start()
+
+        for cc in range(1, len(around) // per):
+
+            @pl.when(c == cc)
+            def _():
+                send_grads(cc - 1)
+
+        @pl.when(c == (len(around) // per) // 2)
+        def _():
+            lo = (len(around) // 2 % per) * BLK
+            grecv[len(around) // 2] = conv[lo : lo + BLK, 0:C].astype(BF16)
+
+    conv[:, 0:C] = scatter(0)(0, jnp.zeros((rows, C), F32))
+    send_grads(len(around) // per - 1)
+
+    @pl.loop(1, G)
+    def _(g):
+        conv[:, 0:C] = scatter(0)(g, conv[:, 0:C])
+
+    for n, (ds, df) in enumerate(around):
+        if ds or df:
+
+            @pl.when(inside(-ds, -df))
+            def _():
+                grad(n, ds, df).wait_recv()
+
+    back = jnp.zeros((BLK, C), F32)
+    for n in range(len(around)):
+        back = back + grecv[n].astype(F32)
+    for b in range(NB):
+        r0 = b * BLK
+        act_b = active[r0 : r0 + BLK]
+        masked, rscale, normed, pre = norm_parts(feat[r0 : r0 + BLK], act_b, gain[...])
+        ag = conv[r0 : r0 + BLK, 0:C] + jnp.where(h == b, back, 0.0)
+        sig = 1.0 / (1.0 + jnp.exp(-pre))
+        ng = ag * sig * (1.0 + pre * (1.0 - sig)) * gain[...]
+        mg = rscale * (ng - normed * jnp.mean(ng * normed, axis=-1, keepdims=True))
+        fgrad[r0 : r0 + BLK] = (
+            (og[r0 : r0 + BLK].astype(F32) * act_b + mg) * act_b
+        ).astype(BF16)
+
+    keep.wait()
+    for d in range(1, S):
+        skip(d).wait()
+    for n, (ds, df) in enumerate(around):
+        if ds or df:
+
+            @pl.when(inside(-ds, -df))
+            def _():
+                halo(n, ds, df).wait_send()
+
+            @pl.when(inside(ds, df))
+            def _():
+                grad(n, ds, df).wait_send()
+
+    @pl.loop(0, G)
+    def _(g):
+        for d in range(1, Z):
+            first(g, d).wait_send()
+
+        @pl.when(g % 2 == 0)
+        def _():
+            for c in [second_a(g)] + third_a(g) + fourth_a(g):
+                c.wait_send()
+
+        @pl.when(g % 2 == 1)
+        def _():
+            for c in [second_b(g)] + third_b(g) + fourth_b(g):
+                c.wait_send()
+
+
+def shards(mesh, features, channel_gain, conv_weight, kernel_map, counts, halo_list, skip_dest, out_grad):
+    S, F = mesh.shape["space"], mesh.shape["fsdp"]
+    koff, cin, width = conv_weight.shape
+    rows, C = features.shape[2:]
+    piece = LANES - width
+    fits = F == 4 and S % 2 == 0 and cin % 16 == 0 and width == Q * piece and halo_list.shape[2] == 1
+    if not (fits and rows == NB * BLK and 9 % NB == 0 and C == F * width):
+        return shards_plain(
+            features, channel_gain, conv_weight, kernel_map, counts, halo_list, skip_dest, out_grad
+        )
+    Z, K4 = S // 2, Q + 1
+    G = -(-koff // K4)
+    slot_ids = jnp.arange(rows, dtype=jnp.int32)
+    active = (slot_ids % BLK < jnp.repeat(counts[0, 0], BLK)).astype(F32)[:, None]
+    w = jnp.pad(conv_weight, ((0, G * K4 - koff), (0, 0), (0, 0))).reshape(G, K4, cin, width)
+    extra = w[:, Q].reshape(G, cin, Q, piece).transpose(0, 2, 1, 3)
+    wire = jnp.concatenate([w[:, :Q], extra], axis=-1)
+    table = rows + 9 * BLK
+    nmap = jnp.pad(kernel_map[0, 0], ((0, G * K4 - koff), (0, 0)), constant_values=table)[:, None, :]
+    owners = skip_dest[0, 0, :, 0]
+    earlier = (owners[None, :] == owners[:, None]) & (slot_ids[None, :] < slot_ids[:, None])
+    placing = jnp.sum(earlier.astype(jnp.int32), axis=1)
+    cap = max(2, 2 * rows // S)
+    tgt = (owners * cap + placing)[None, :]
+    vm = pl.BlockSpec(memory_space=pltpu.VMEM)
+    dma = pltpu.SemaphoreType.DMA
+    sec, fgrad, recv = pl.pallas_call(
+        functools.partial(section_kernel, (S, F, Z, G, K4)),
+        out_shape=(
+            jax.ShapeDtypeStruct((rows, C), BF16),
+            jax.ShapeDtypeStruct((rows, C), BF16),
+            jax.ShapeDtypeStruct((S, cap, C), BF16),
+        ),
+        in_specs=[pl.BlockSpec(memory_space=pltpu.SMEM)] + [vm] * 7,
+        out_specs=(vm, vm, vm),
+        scratch_shapes=[
+            pltpu.VMEM((G, F, Q, Z, 2, cin, LANES), BF16),
+            pltpu.VMEM((table, C), BF16),
+            pltpu.VMEM((G * K4, rows, C), BF16),
+            pltpu.VMEM((rows, F * LANES), F32),
+            pltpu.VMEM((BLK, C), BF16),
+            pltpu.VMEM((rows, F * LANES), BF16),
+            pltpu.VMEM((C, F * LANES), BF16),
+            pltpu.VMEM((9, BLK, C), BF16),
+            pltpu.VMEM((9, BLK, C), BF16),
+            pltpu.VMEM((S, cap, C), BF16),
+            dma((G, Z + 4)),
+            dma((G, Z + 4)),
+            dma((9,)),
+            dma((9,)),
+            dma((S - 1,)),
+            dma((S - 1,)),
+            dma((9,)),
+            dma((9,)),
+            dma,
+        ],
+        compiler_params=pltpu.CompilerParams(collective_id=0, has_side_effects=True),
+        name="section",
+    )(halo_list[0, 0], features[0, 0], channel_gain[None, :], active, out_grad[0, 0], wire, nmap, tgt)
+    return (sec[None, None], fgrad[None, None], recv[None, None])
+
+
 def solution(mesh):
     return jax.shard_map(
-        shards,
+        functools.partial(shards, mesh),
         mesh=mesh,
         in_specs=(
             P("space", "fsdp", None, None),

time: 632 us -> 131 us (0.21)
  blocking collectives: 341 us -> 0 us
  Pallas kernels: 0 us -> 119 us
  other arithmetic: 121 us -> 3.71 us
  local copies, waits for them, and re-layouts: 78.1 us -> 5.92 us
  matrix products: 42.5 us -> 0 us
  starting transfers between devices: 38 us -> 0 us
    all_gather x18 -> x0, blocking collectives: 341 us -> none  [the longest x9 240 us: group_step(): full_weights = lax.all_gather(widened, 'space', axis=1, tiled=True)]
    pallas_call x0 -> x1, Pallas kernels: none -> 119 us  [shards(): pl.pallas_call(functools.partial(section_kernel, (S, F, Z, G, K4)), out_s...]
    scatter-add x10 -> x0, other arithmetic: 99.6 us -> none  [the longest x9 98.9 us: group_step(): table_grad.at[neighbours.reshape(-1)].add(backward.reshape(-1, width))]
    gather x9 -> x0, local copies, waits for them, and re-layouts: 52 us -> none  [group_step(): picked = lookup[neighbours]]
    dot_general x18 -> x0, matrix products: 42.5 us -> none  [the longest x9 25.4 us: group_step(): jnp.einsum('kvc,kcd->vd', picked, full_weights, preferred_element_type=jn...]
    ppermute x8 -> x0, starting transfers between devices: 29.7 us -> none  [the longest x4 17.8 us: passed_along(): return lax.ppermute(x, axis, pairs)]
    all_to_all x1 -> x0, starting transfers between devices: 8.25 us -> none  [shards(): lax.all_to_all(outbox.reshape(space_size, capacity, width), 'space', spli...]
    dynamic_slice x18 -> x0, local copies, waits for them, and re-layouts: 8.05 us -> none  [shards(): lax.scan(group_step, start, (weight_groups, map_groups))]
  transfers between devices with their start and end apart: 9 -> 0, of which waited for: 4 -> 0; matrix products, arithmetic and copies ran while one was open for 2% -> 0% of each run, Pallas kernels for 0% -> 0%
where the time goes in v1:
time: 131 us
  Pallas kernels  119 us (91%)
  local copies, waits for them, and re-layouts  5.92 us (5%)
  other arithmetic  3.71 us (3%)
  between operations  1.44 us (1%)
    pallas_call x1, Pallas kernels, shards(): pl.pallas_call(functools.partial(section_kernel, (S, F, Z, G, K4)), out_s...  119 us
    unnamed x15, local copies, waits for them, and re-layouts  3.41 us

profile of v1, /device:TPU:13, one launch (start us, length us, event | category | flops | bytes accessed | tf_op | source)
XLA Modules:
  0.0 130.5 jit_solution(4790629196514456360)
XLA Ops:
  0.6 0.0 copy-start
  0.6 0.0 copy-start.4
  0.7 0.0 copy-start.2
  1.4 0.0 copy-done
  1.4 1.2 broadcast_in_dim.22.gain
  2.6 0.1 broadcast_bitcast_fusion
  2.7 0.7 reduce
  3.4 0.2 convert_reduce_fusion
  3.6 1.2 bitcast_add_fusion.tgt
  4.9 0.2 copy.17
  5.0 0.0 copy-done.4
  5.1 0.6 broadcast_in_dim.24.nmap
  5.7 0.7 convert_element_type.15.active
  6.4 0.0 copy-done.2
  6.4 0.1 pad.8
  6.5 0.1 copy.18
  6.7 0.2 copy.19
  6.9 0.8 pad_maximum_fusion.wire
  7.7 119.5 %section.1 = (bf16[384,384]{1,0:T(8,128)(2,1)}, bf16[384,384]{1,0:T(8,128)(2,1)}, bf16[8,96,384]{2,1,0:T(8,128)(2,1)}) custom-call(s32[1]{0:T(128)} %bitcast.21.h_ref, bf16[384,384]{1,0:T(8,128)(2,1)} %bitcast.28, f32[1,384]{1,0:T(1,128)} %broadcast_in_dim.22.gain, f32[384,1]{1,0:T(8,128)} %convert_element_type.15.active, bf16[384,384]{1,0:T(8,128)(2,1)} %bitcast.29, ...), custom_call_target="tpu_custom_call" | custom-call | tf_op jit(solution)/shard_map/section/pallas_call | solution.py:533
  127.2 0.0 copy-start.3
  127.2 0.0 copy-start.1
  127.2 1.8 %copy.29 = bf16[1,1,384,384]{3,2,1,0:T(8,128)(2,1)} copy(bf16[1,1,384,384]{3,2,1,0:T(8,128)(2,1)} %bitcast.31) | data formatting | bytes 589824
  129.0 0.0 copy-done.3
  129.0 0.7 copy.30
  129.7 0.0 copy-done.1
  129.7 0.8 copy.31
  (5 shorter events, 0.1 us)
Async XLA Ops:
  0.6 0.7 copy-start
  0.6 4.4 %copy-start.4 = (s32[1,1,27,384]{3,1,2,0:T(1,128)S(1)}, s32[1,1,27,384]{3,1,2,0:T(1,128)}, u32[]{:S(2)}) copy-start(s32[1,1,27,384]{3,1,2,0:T(1,128)} %param.11) | copy-start | bytes 124420
  0.7 5.8 %copy-start.2 = (bf16[27,48,96]{2,1,0:T(8,128)(2,1)S(1)}, bf16[27,48,96]{2,1,0:T(8,128)(2,1)}, u32[]{:S(2)}) copy-start(bf16[27,48,96]{2,1,0:T(8,128)(2,1)} %param.10) | copy-start | bytes 746500
  127.2 1.8 %copy-start.3 = (bf16[384,384]{1,0:T(8,128)(2,1)S(1)}, bf16[384,384]{1,0:T(8,128)(2,1)}, u32[]{:S(2)}) copy-start(bf16[384,384]{1,0:T(8,128)(2,1)} %get-tuple-element.7) | copy-start | bytes 884740
  127.2 2.5 %copy-start.1 = (bf16[8,96,384]{2,1,0:T(8,128)(2,1)S(1)}, bf16[8,96,384]{2,1,0:T(8,128)(2,1)}, u32[]{:S(2)}) copy-start(bf16[8,96,384]{2,1,0:T(8,128)(2,1)} %get-tuple-element.8) | copy-start | bytes 1769476

commit v2 on v1

--- a/solution.py
+++ b/solution.py
@@ -158,9 +158,9 @@
 
 
 def section_kernel(
-    dims, h_ref, feat, gain, active, og, wire, nmap, tgt,
+    dims, h_ref, counts, feat, gain, og, wire, maps, owners,
     sec, fgrad, recv,
-    wbuf, lookup, pb, conv, shared, rgp, w3, gsend, grecv, outbox,
+    active, nmap, tgt, wbuf, lookup, pb, conv, shared, rgp, w3, gsend, grecv, outbox,
     wsend, wrecv, hsend, hrecv, ssend, srecv, bsend, brecv, own_sem,
 ):
     S, F, Z, G, K4 = dims
@@ -187,7 +187,20 @@
 
     own = pltpu.make_async_copy(wire, wbuf.at[:, f, :, z, y], own_sem)
     own.start()
-    masked, rscale, normed, pre = norm_parts(feat[...], active[...], gain[...])
+    slot = lax.broadcasted_iota(jnp.int32, (BLK, 1), 0)
+    for b in range(NB):
+        active[b * BLK : (b + 1) * BLK] = jnp.where(slot < counts[b], 1.0, 0.0)
+    gains = gain[...].reshape(1, C)
+    koff = maps.shape[0]
+    nmap[0:koff] = maps[...]
+    nmap[koff:] = jnp.full((nmap.shape[0] - koff, rows), table, jnp.int32)
+    owner_row = owners[...]
+    owner_col = jnp.transpose(jnp.broadcast_to(owner_row, (8, rows)))[:, 0:1]
+    row_at = lax.broadcasted_iota(jnp.int32, (rows, rows), 0)
+    col_at = lax.broadcasted_iota(jnp.int32, (rows, rows), 1)
+    earlier = jnp.where((owner_row == owner_col) & (row_at < col_at), 1, 0)
+    tgt[...] = owner_row * recv.shape[1] + jnp.sum(earlier, axis=0, keepdims=True)
+    masked, rscale, normed, pre = norm_parts(feat[...], active[...], gains)
     act = (pre / (1.0 + jnp.exp(-pre))).astype(BF16)
     lookup[0:rows, :] = act
     h = h_ref[0]
@@ -237,34 +250,33 @@
             ((z + d) % Z) * Y + y, f,
         )
 
-    def strip(g, col, i, ss, ff):
-        ref = wbuf.at[g, col, :, :, y]
+    def passed(ref, g, i, ss, ff):
         return remote(ref, ref, wsend.at[g, i], wrecv.at[g, i], ss, ff)
 
-    def column(g, col, i, ss, ff):
-        ref = wbuf.at[g, col]
-        return remote(ref, ref, wsend.at[g, i], wrecv.at[g, i], ss, ff)
-
     B0 = Z - 1
-
-    def second_a(g):
-        return strip(g, f, B0, sy, f)
-
-    def second_b(g):
-        return strip(g, f, B0, s, fx)
-
-    def third_a(g):
-        return [column(g, f, B0 + 1, s, fx), column(g, f, B0 + 2, s, fp)]
-
-    def third_b(g):
-        return [strip(g, f, B0 + 1, sy, f), strip(g, fx, B0 + 4, sy, f)]
-
-    def fourth_a(g):
-        return [column(g, fx, B0 + 3, s, fp)]
-
-    def fourth_b(g):
-        return [column(g, f, B0 + 2, s, fp), column(g, fx, B0 + 3, s, fp)]
-
+    low, high = pl.ds(0, Z // 2), pl.ds(Z // 2, Z - Z // 2)
+
+    def second(g):
+        return [
+            passed(wbuf.at[g, f, :, low, y], g, B0, sy, f),
+            passed(wbuf.at[g, f, :, high, y], g, B0 + 1, s, fx),
+        ]
+
+    def third(g):
+        return [
+            passed(wbuf.at[g, f, :, low], g, B0 + 2, s, fx),
+            passed(wbuf.at[g, f, :, high, y], g, B0 + 3, sy, f),
+            passed(wbuf.at[g, fx, :, high, y], g, B0 + 4, sy, f),
+        ]
+
+    def fourth(g):
+        return [
+            passed(wbuf.at[g, f], g, B0 + 5, s, fp),
+            passed(wbuf.at[g, fx], g, B0 + 6, s, fp),
+        ]
+
+    for d in range(1, Z):
+        first(0, d).start()
     for n, (ds, df) in enumerate(around):
         if ds or df:
 
@@ -272,23 +284,17 @@
             def _():
                 halo(n, ds, df).start()
 
-    @pl.loop(0, G)
+    @pl.loop(1, G)
     def _(g):
         for d in range(1, Z):
             first(g, d).start()
 
     own.wait()
-    for n, (ds, df) in enumerate(around):
-        if ds or df:
-
-            @pl.when(inside(ds, df))
-            def _():
-                halo(n, ds, df).wait_recv()
 
     lane_u = lax.broadcasted_iota(jnp.int32, (rows, table), 1)
 
     def gather(k):
-        line = jnp.broadcast_to(nmap[k], (8, rows))
+        line = jnp.broadcast_to(nmap[pl.ds(k, 1)], (8, rows))
         ids = jnp.transpose(line)[:, 0:1]
         pick = jnp.where(lane_u == ids, 1.0, 0.0).astype(BF16)
         pb[k] = jnp.dot(pick, lookup[...], preferred_element_type=F32).astype(BF16)
@@ -310,58 +316,43 @@
             for d in range(1, Z):
                 first(t, d).wait_recv()
 
-            @pl.when(t % 2 == 0)
-            def _():
-                second_a(t).start()
-
-            @pl.when(t % 2 == 1)
-            def _():
-                second_b(t).start()
-
-        g3 = t - 1
-
-        @pl.when((g3 >= 0) & (g3 < G))
-        def _():
-            @pl.when(g3 % 2 == 0)
-            def _():
-                second_a(g3).wait_recv()
-                for c in third_a(g3):
-                    c.start()
-
-            @pl.when(g3 % 2 == 1)
-            def _():
-                second_b(g3).wait_recv()
-                for c in third_b(g3):
-                    c.start()
-
-        g4 = t - 2
-
-        @pl.when((g4 >= 0) & (g4 < G))
-        def _():
-            @pl.when(g4 % 2 == 0)
-            def _():
-                third_a(g4)[0].wait_recv()
-                for c in fourth_a(g4):
-                    c.start()
-
-            @pl.when(g4 % 2 == 1)
-            def _():
-                for c in third_b(g4):
-                    c.wait_recv()
-                for c in fourth_b(g4):
-                    c.start()
-
-        @pl.when(t < G)
+            for c in second(t):
+                c.start()
+
+        @pl.when((t >= 1) & (t < G + 1))
+        def _():
+            for c in second(t - 1):
+                c.wait_recv()
+            for c in third(t - 1):
+                c.start()
+
+        @pl.when((t >= 2) & (t < G + 2))
+        def _():
+            for c in third(t - 2):
+                c.wait_recv()
+            for c in fourth(t - 2):
+                c.start()
+
+        @pl.when(t == 1)
+        def _():
+            for n, (ds, df) in enumerate(around):
+                if ds or df:
+
+                    @pl.when(inside(ds, df))
+                    def _():
+                        halo(n, ds, df).wait_recv()
+
+        @pl.when((t >= 1) & (t < G + 1))
         def _():
             @pl.loop(0, K4)
             def _(j):
-                gather(t * K4 + j)
+                gather((t - 1) * K4 + j)
 
         g5 = t - 3
 
         @pl.when(g5 >= 0)
         def _():
-            for c in fourth_b(g5):
+            for c in fourth(g5):
                 c.wait_recv()
             lanes = lax.broadcasted_iota(jnp.int32, (C, LANES), 1)
             piece = LANES - width
@@ -394,7 +385,7 @@
         def step(g, acc):
             base = lax.broadcasted_iota(jnp.int32, (rows, rows), 0) + u0
             hot = jnp.concatenate(
-                [jnp.where(base == nmap[g * K4 + j], 1.0, 0.0).astype(BF16) for j in range(K4)], axis=1
+                [jnp.where(base == nmap[pl.ds(g * K4 + j, 1)], 1.0, 0.0).astype(BF16) for j in range(K4)], axis=1
             )
             return acc + jnp.dot(
                 hot, pb[pl.ds(g * K4, K4)].reshape(K4 * rows, C), preferred_element_type=F32
@@ -465,10 +456,10 @@
     for b in range(NB):
         r0 = b * BLK
         act_b = active[r0 : r0 + BLK]
-        masked, rscale, normed, pre = norm_parts(feat[r0 : r0 + BLK], act_b, gain[...])
+        masked, rscale, normed, pre = norm_parts(feat[r0 : r0 + BLK], act_b, gains)
         ag = conv[r0 : r0 + BLK, 0:C] + jnp.where(h == b, back, 0.0)
         sig = 1.0 / (1.0 + jnp.exp(-pre))
-        ng = ag * sig * (1.0 + pre * (1.0 - sig)) * gain[...]
+        ng = ag * sig * (1.0 + pre * (1.0 - sig)) * gains
         mg = rscale * (ng - normed * jnp.mean(ng * normed, axis=-1, keepdims=True))
         fgrad[r0 : r0 + BLK] = (
             (og[r0 : r0 + BLK].astype(F32) * act_b + mg) * act_b
@@ -493,15 +484,8 @@
         for d in range(1, Z):
             first(g, d).wait_send()
 
-        @pl.when(g % 2 == 0)
-        def _():
-            for c in [second_a(g)] + third_a(g) + fourth_a(g):
-                c.wait_send()
-
-        @pl.when(g % 2 == 1)
-        def _():
-            for c in [second_b(g)] + third_b(g) + fourth_b(g):
-                c.wait_send()
+        for c in second(g) + third(g) + fourth(g):
+            c.wait_send()
 
 
 def shards(mesh, features, channel_gain, conv_weight, kernel_map, counts, halo_list, skip_dest, out_grad):
@@ -516,18 +500,12 @@
         )
     Z, K4 = S // 2, Q + 1
     G = -(-koff // K4)
-    slot_ids = jnp.arange(rows, dtype=jnp.int32)
-    active = (slot_ids % BLK < jnp.repeat(counts[0, 0], BLK)).astype(F32)[:, None]
     w = jnp.pad(conv_weight, ((0, G * K4 - koff), (0, 0), (0, 0))).reshape(G, K4, cin, width)
     extra = w[:, Q].reshape(G, cin, Q, piece).transpose(0, 2, 1, 3)
     wire = jnp.concatenate([w[:, :Q], extra], axis=-1)
     table = rows + 9 * BLK
-    nmap = jnp.pad(kernel_map[0, 0], ((0, G * K4 - koff), (0, 0)), constant_values=table)[:, None, :]
-    owners = skip_dest[0, 0, :, 0]
-    earlier = (owners[None, :] == owners[:, None]) & (slot_ids[None, :] < slot_ids[:, None])
-    placing = jnp.sum(earlier.astype(jnp.int32), axis=1)
     cap = max(2, 2 * rows // S)
-    tgt = (owners * cap + placing)[None, :]
+    owners = skip_dest[0, 0].reshape(1, rows)
     vm = pl.BlockSpec(memory_space=pltpu.VMEM)
     dma = pltpu.SemaphoreType.DMA
     sec, fgrad, recv = pl.pallas_call(
@@ -537,9 +515,12 @@
             jax.ShapeDtypeStruct((rows, C), BF16),
             jax.ShapeDtypeStruct((S, cap, C), BF16),
         ),
-        in_specs=[pl.BlockSpec(memory_space=pltpu.SMEM)] + [vm] * 7,
+        in_specs=[pl.BlockSpec(memory_space=pltpu.SMEM)] * 2 + [vm] * 6,
         out_specs=(vm, vm, vm),
         scratch_shapes=[
+            pltpu.VMEM((rows, 1), F32),
+            pltpu.VMEM((G * K4, rows), jnp.int32),
+            pltpu.VMEM((1, rows), jnp.int32),
             pltpu.VMEM((G, F, Q, Z, 2, cin, LANES), BF16),
             pltpu.VMEM((table, C), BF16),
             pltpu.VMEM((G * K4, rows, C), BF16),
@@ -550,8 +531,8 @@
             pltpu.VMEM((9, BLK, C), BF16),
             pltpu.VMEM((9, BLK, C), BF16),
             pltpu.VMEM((S, cap, C), BF16),
-            dma((G, Z + 4)),
-            dma((G, Z + 4)),
+            dma((G, Z + 6)),
+            dma((G, Z + 6)),
             dma((9,)),
             dma((9,)),
             dma((S - 1,)),
@@ -562,7 +543,9 @@
         ],
         compiler_params=pltpu.CompilerParams(collective_id=0, has_side_effects=True),
         name="section",
-    )(halo_list[0, 0], features[0, 0], channel_gain[None, :], active, out_grad[0, 0], wire, nmap, tgt)
+    )(
+        halo_list[0, 0], counts[0, 0], features[0, 0], channel_gain, out_grad[0, 0], wire, kernel_map[0, 0], owners
+    )
     return (sec[None, None], fgrad[None, None], recv[None, None])
 
 

time: 131 us -> 119 us (0.908); the launches traced: 131 us -> 117 us
  Pallas kernels: 119 us -> 109 us
  other arithmetic: 3.71 us -> 0.85 us
    pallas_call x1, Pallas kernels: 119 us -> 109 us  [shards(): pl.pallas_call(functools.partial(section_kernel, (S, F, Z, G, K4)), out_s...]
    broadcast_in_dim x2 -> x0, local copies, waits for them, and re-layouts: 1.9 us -> none  [the longest x1 1.25 us: shards(): channel_gain[None, :]]
    unnamed x15 -> x8, local copies, waits for them, and re-layouts: 3.41 us -> 4.72 us
where the time goes in v2:
time: 119 us; the launch traced here: 117 us
  Pallas kernels  109 us (92%)
  local copies, waits for them, and re-layouts  6.13 us (5%)
  between operations  1.33 us (1%)
    pallas_call x1, Pallas kernels, shards(): pl.pallas_call(functools.partial(section_kernel, (S, F, Z, G, K4)), out_s...  109 us
    unnamed x8, local copies, waits for them, and re-layouts  4.72 us

profile of v2, /device:TPU:13, one launch (start us, length us, event | category | flops | bytes accessed | tf_op | source)
XLA Modules:
  0.0 117.1 jit_solution(12814050488537177515)
XLA Ops:
  1.3 1.4 %copy.15 = s32[1,1,27,384]{3,2,1,0:T(8,128)} copy(s32[1,1,27,384]{3,1,2,0:T(1,128)} %param.11) | data formatting | bytes 82944
  2.7 1.0 pad.4
  3.8 0.1 copy.11
  3.9 0.2 copy.12
  4.1 0.8 pad_maximum_fusion.wire
  5.0 108.8 %section.1 = (bf16[384,384]{1,0:T(8,128)(2,1)}, bf16[384,384]{1,0:T(8,128)(2,1)}, bf16[8,96,384]{2,1,0:T(8,128)(2,1)}) custom-call(s32[1]{0:T(128)} %bitcast.14.h_ref, s32[3]{0:T(128)} %bitcast.26, bf16[384,384]{1,0:T(8,128)(2,1)} %bitcast.20, f32[384]{0:T(512)} %gain.1, bf16[384,384]{1,0:T(8,128)(2,1)} %bitcast.21, ...), custom_call_target="tpu_custom_call" | custom-call | tf_op jit(solution)/shard_map/section/pallas_call | solution.py:511
  113.8 0.0 copy-start.1
  113.8 0.0 copy-start
  113.8 1.8 %copy.20 = bf16[1,1,384,384]{3,2,1,0:T(8,128)(2,1)} copy(bf16[1,1,384,384]{3,2,1,0:T(8,128)(2,1)} %bitcast.23) | data formatting | bytes 589824
  115.6 0.0 copy-done.1
  115.6 0.7 copy.21
  116.3 0.0 copy-done
  116.3 0.8 copy.22
  (2 shorter events, 0.0 us)
Async XLA Ops:
  113.8 1.8 %copy-start.1 = (bf16[384,384]{1,0:T(8,128)(2,1)S(1)}, bf16[384,384]{1,0:T(8,128)(2,1)}, u32[]{:S(2)}) copy-start(bf16[384,384]{1,0:T(8,128)(2,1)} %get-tuple-element.7) | copy-start | bytes 884740
  113.8 2.5 %copy-start = (bf16[8,96,384]{2,1,0:T(8,128)(2,1)S(1)}, bf16[8,96,384]{2,1,0:T(8,128)(2,1)}, u32[]{:S(2)}) copy-start(bf16[8,96,384]{2,1,0:T(8,128)(2,1)} %get-tuple-element.8) | copy-start | bytes 1769476

commit v3 on v2

--- a/solution.py
+++ b/solution.py
@@ -417,13 +417,13 @@
         def _(g):
             conv[:, 0:C] = scatter((c + 1) * rows)(g, conv[:, 0:C])
 
+            @pl.when((c == 0) & (g == 0))
+            def _():
+                for d in range(1, S):
+                    skip(d).start()
+                keep.start()
+
         gsend[pl.ds(c * per, per)] = conv[:, 0:C].astype(BF16).reshape(per, BLK, C)
-
-        @pl.when(c == 0)
-        def _():
-            for d in range(1, S):
-                skip(d).start()
-            keep.start()
 
         for cc in range(1, len(around) // per):
 

time: 119 us -> 117 us (0.983)
  Pallas kernels: 109 us -> 107 us
    pallas_call x1, Pallas kernels: 109 us -> 107 us  [shards(): pl.pallas_call(functools.partial(section_kernel, (S, F, Z, G, K4)), out_s...]
where the time goes in v3:
time: 117 us; the launch traced here: 116 us
  Pallas kernels  107 us (91%)
  local copies, waits for them, and re-layouts  6.13 us (5%)
  between operations  1.33 us (1%)
    pallas_call x1, Pallas kernels, shards(): pl.pallas_call(functools.partial(section_kernel, (S, F, Z, G, K4)), out_s...  107 us
    unnamed x8, local copies, waits for them, and re-layouts  4.72 us

profile of v3, /device:TPU:13, one launch (start us, length us, event | category | flops | bytes accessed | tf_op | source)
XLA Modules:
  0.0 115.5 jit_solution(5239488283491727359)
XLA Ops:
  1.3 1.4 %copy.15 = s32[1,1,27,384]{3,2,1,0:T(8,128)} copy(s32[1,1,27,384]{3,1,2,0:T(1,128)} %param.11) | data formatting | bytes 82944
  2.7 1.0 pad.4
  3.8 0.1 copy.11
  3.9 0.2 copy.12
  4.1 0.8 pad_maximum_fusion.wire
  5.0 107.2 %section.1 = (bf16[384,384]{1,0:T(8,128)(2,1)}, bf16[384,384]{1,0:T(8,128)(2,1)}, bf16[8,96,384]{2,1,0:T(8,128)(2,1)}) custom-call(s32[1]{0:T(128)} %bitcast.14.h_ref, s32[3]{0:T(128)} %bitcast.26, bf16[384,384]{1,0:T(8,128)(2,1)} %bitcast.20, f32[384]{0:T(512)} %gain.1, bf16[384,384]{1,0:T(8,128)(2,1)} %bitcast.21, ...), custom_call_target="tpu_custom_call" | custom-call | tf_op jit(solution)/shard_map/section/pallas_call | solution.py:511
  112.2 0.0 copy-start.1
  112.2 0.0 copy-start
  112.2 1.8 %copy.20 = bf16[1,1,384,384]{3,2,1,0:T(8,128)(2,1)} copy(bf16[1,1,384,384]{3,2,1,0:T(8,128)(2,1)} %bitcast.23) | data formatting | bytes 589824
  114.0 0.0 copy-done.1
  114.0 0.7 copy.21
  114.7 0.0 copy-done
  114.7 0.8 copy.22
  (2 shorter events, 0.0 us)
Async XLA Ops:
  112.2 1.8 %copy-start.1 = (bf16[384,384]{1,0:T(8,128)(2,1)S(1)}, bf16[384,384]{1,0:T(8,128)(2,1)}, u32[]{:S(2)}) copy-start(bf16[384,384]{1,0:T(8,128)(2,1)} %get-tuple-element.7) | copy-start | bytes 884740
  112.2 2.5 %copy-start = (bf16[8,96,384]{2,1,0:T(8,128)(2,1)S(1)}, bf16[8,96,384]{2,1,0:T(8,128)(2,1)}, u32[]{:S(2)}) copy-start(bf16[8,96,384]{2,1,0:T(8,128)(2,1)} %get-tuple-element.8) | copy-start | bytes 1769476
